TPU v7x, 256 devices: a whole 4x4x8 slice. The times are simulated.
256 devices in a mesh: req: 32 (over y, x, core), head: 8 (over z).
Axes of the slice: x: 4, y: 4, z: 8, core: 2. Of those that a mesh axis runs over, the one named last changes fastest.
Arguments:
- tokens: bfloat16 [4096, 1536], P(('req', 'head')), may hold values from -6 to 6
- pre_gain: float32 [1536], replicated, may hold values from 0.1 to 1.9
- inner_weight: bfloat16 [1536, 2, 3072], P(None, None, 'head')
- shared_weight: bfloat16 [1536, 304], replicated, may hold values from -0.15625 to 0.15625
- conv_inner: float32 [4, 3072], P(None, 'head'), may hold values from -0.5 to 0.5
- conv_inner_bias: float32 [3072], P('head'), may hold values from -0.5 to 0.5
- conv_shared: float32 [4, 256], replicated, may hold values from -0.5 to 0.5
- conv_shared_bias: float32 [256], replicated, may hold values from -0.5 to 0.5
- step_bias: float32 [48], P('head'), may hold values from -4 to 0
- decay_log: float32 [48], P('head'), may hold values from 0 to 2.77
- skip_gain: float32 [48], P('head'), may hold values from 0.5 to 1.5
- gate_gain: float32 [3072], P('head'), may hold values from 0.1 to 1.9
- out_weight: bfloat16 [3072, 1536], P('head'), may hold values from -0.109375 to 0.109375
- states: bfloat16 [1024, 48, 64, 128], P('req', 'head'), may hold values from -1.1953125 to 1.1953125
- edge_inner: bfloat16 [1024, 3, 3072], P('req', None, 'head'), may hold values from -6 to 6
- edge_shared: bfloat16 [1024, 3, 256], P('req'), may hold values from -6 to 6
- counts: int32 [1024], P('req'), may hold values from 1 to 4, as said below
- mig_ids: int32 [32], replicated, may hold values from 0 to 1023, as said below
- mig_dest: int32 [32], replicated, may hold values from 0 to 1023, as said below
- reorder: int32 [1024], replicated, may hold values from 0 to 1023, as said below
Outputs:
- hidden_out: bfloat16 [4096, 1536], P(('req', 'head'))
- states_out: bfloat16 [1024, 48, 64, 128], P('req', 'head')
- edge_inner_out: bfloat16 [1024, 3, 3072], P('req', None, 'head')
- edge_shared_out: bfloat16 [1024, 3, 256], P('req')
Inputs may be any that keep to these rules, and one draw needn't show every extreme that they name: counts: each slot's token rows are r * 4 to r * 4 + 3 of tokens; the first counts[r] of them are real. mig_ids: distinct old slots listed by owner: entry i is one of the slots i * 32 to (i + 1) * 32 - 1, those held by index i of req. mig_dest: a reordering of the slots in mig_ids. reorder: a permutation of all slots. The 32 new slots j with j // 32 = d take at most 1 values reorder[j] of any one block of 32 slots, and exactly 1 of some block.
All inputs are finite; a program needn't handle non-finite values.
Results may differ from a plain program's by a relative error of at most 0.013.
Values may be sent and summed in bfloat16 or wider, within the bound.
A program may use at most 128 MiB of HBM per device.

v0:
```python
import jax
import jax.numpy as jnp
from jax import lax
from jax.sharding import PartitionSpec as P

EPS = 1e-05


def advance(carried, step_now, inputs_now, entry_now, readout_now, decay, skip_gain):
    factor = jnp.exp(step_now * decay)
    carried = (
        carried * factor[:, :, None, None]
        + (step_now[:, :, None] * inputs_now)[:, :, :, None] * entry_now[:, None, None, :]
    )
    produced = jnp.einsum("khpn,kn->khp", carried, readout_now, precision=lax.Precision.HIGHEST)
    return (carried, produced + skip_gain[None, :, None] * inputs_now)


def depthwise(edge, fresh, weight, offset_bias):
    sequence = jnp.concatenate([edge, fresh], axis=1).astype(jnp.float32)
    window = fresh.shape[1]
    summed = sequence[:, 0:window] * weight[0]
    for offset in range(1, weight.shape[0]):
        summed = summed + sequence[:, offset : offset + window] * weight[offset]
    return jax.nn.silu(summed + offset_bias)


def new_edge(edge, fresh, counts):
    sequence = jnp.concatenate([edge, fresh], axis=1)
    keep_rows = edge.shape[1]
    result = edge
    for length in range(1, fresh.shape[1] + 1):
        result = jnp.where(
            (counts == length)[:, None, None], sequence[:, length : length + keep_rows], result
        )
    return result


def rank_rows(partner, position, capacity):
    matching = partner[:, None] == partner[None, :]
    earlier = position[None, :] < position[:, None]
    ranking = jnp.sum(jnp.logical_and(matching, earlier), axis=1)
    return partner * capacity + ranking


def pack_pages(member, send_rows, buffer_rows):
    empty = jnp.zeros((buffer_rows,) + member.shape[1:], member.dtype)
    return empty.at[send_rows].set(member)


def route_rows(anchor, first_slot, slot_count, all_slots, capacity):
    inverse = jnp.zeros(all_slots.shape, jnp.int32).at[anchor].set(all_slots)
    targets = lax.dynamic_slice_in_dim(inverse, first_slot, slot_count)
    send_rows = rank_rows(targets // slot_count, targets % slot_count, capacity)
    sources = lax.dynamic_slice_in_dim(anchor, first_slot, slot_count)
    recv_rows = rank_rows(sources // slot_count, jnp.arange(slot_count, dtype=jnp.int32), capacity)
    return (send_rows, recv_rows)


def local(
    tokens,
    pre_gain,
    inner_weight,
    shared_weight,
    conv_inner,
    conv_inner_bias,
    conv_shared,
    conv_shared_bias,
    step_bias,
    decay_log,
    skip_gain,
    gate_gain,
    out_weight,
    states,
    edge_inner,
    edge_shared,
    counts,
    mig_ids,
    mig_dest,
    reorder,
):
    slot_count = states.shape[0]
    heads_here = states.shape[1]
    head_dim = states.shape[2]
    state_dim = states.shape[3]
    inner_here = heads_here * head_dim
    groups = lax.axis_size("req")
    device = lax.axis_index("req")
    first_slot = device * slot_count
    moving = mig_ids.shape[0] // groups
    stride = (slot_count + groups - 1) // groups
    all_slots = jnp.arange(slot_count * groups, dtype=jnp.int32)
    rows_in = tokens.astype(jnp.float32)
    normed = (
        rows_in * lax.rsqrt(jnp.mean(rows_in * rows_in, axis=-1, keepdims=True) + EPS) * pre_gain
    ).astype(jnp.bfloat16)
    inner_flat = inner_weight.reshape(inner_weight.shape[0], 2 * inner_here)
    piece_rows = lax.all_gather(normed, "head", axis=0, tiled=True)
    inner_rows = jnp.dot(piece_rows, inner_flat, preferred_element_type=jnp.float32).astype(
        jnp.bfloat16
    )
    shared_rows = jnp.dot(piece_rows, shared_weight, preferred_element_type=jnp.float32).astype(
        jnp.bfloat16
    )
    projected = jnp.concatenate([inner_rows, shared_rows], axis=1)
    own_ids = lax.dynamic_slice_in_dim(mig_ids, device * moving, moving)
    local_ids = own_ids - first_slot
    arrived = (
        lax.all_gather(states[local_ids], "req", axis=0, tiled=True),
        lax.all_gather(edge_inner[local_ids], "req", axis=0, tiled=True),
        lax.all_gather(edge_shared[local_ids], "req", axis=0, tiled=True),
    )
    picked = jnp.argmax(mig_dest[None, :] == own_ids[:, None], axis=1)
    sectioned_states = states.at[local_ids].set(arrived[0][picked])
    sectioned_inner = edge_inner.at[local_ids].set(arrived[1][picked])
    sectioned_shared = edge_shared.at[local_ids].set(arrived[2][picked])
    send_rows, recv_rows = route_rows(reorder, first_slot, slot_count, all_slots, stride)
    buffer_rows = groups * stride
    received = (
        lax.all_to_all(
            pack_pages(sectioned_states, send_rows, buffer_rows),
            "req",
            split_axis=0,
            concat_axis=0,
            tiled=True,
        ),
        lax.all_to_all(
            pack_pages(sectioned_inner, send_rows, buffer_rows),
            "req",
            split_axis=0,
            concat_axis=0,
            tiled=True,
        ),
        lax.all_to_all(
            pack_pages(sectioned_shared, send_rows, buffer_rows),
            "req",
            split_axis=0,
            concat_axis=0,
            tiled=True,
        ),
    )
    moved_states = received[0][recv_rows]
    moved_inner = received[1][recv_rows]
    moved_shared = received[2][recv_rows]
    window = projected.shape[0] // slot_count
    projected = projected.reshape(slot_count, window, projected.shape[1])
    gate_part = projected[:, :, :inner_here]
    value_part = projected[:, :, inner_here : 2 * inner_here]
    fresh_shared = projected[:, :, 2 * inner_here : 2 * inner_here + 2 * state_dim]
    head_index = lax.axis_index("head")
    step_raw = lax.dynamic_slice_in_dim(
        projected[:, :, 2 * inner_here + 2 * state_dim :],
        head_index * heads_here,
        heads_here,
        axis=2,
    )
    edge_inner_out = new_edge(moved_inner, value_part, counts)
    edge_shared_out = new_edge(moved_shared, fresh_shared, counts)
    mixed_inner = depthwise(moved_inner, value_part, conv_inner, conv_inner_bias)
    mixed_shared = depthwise(moved_shared, fresh_shared, conv_shared, conv_shared_bias)
    valid = jnp.arange(window)[None, :] < counts[:, None]
    step_size = jax.nn.softplus(step_raw.astype(jnp.float32) + step_bias)
    step_size = jnp.where(valid[:, :, None], step_size, 0.0)
    decay = -jnp.exp(decay_log)
    inputs = mixed_inner.reshape(slot_count, window, heads_here, head_dim)
    entries = mixed_shared[:, :, :state_dim]
    readouts = mixed_shared[:, :, state_dim:]
    carried = moved_states.astype(jnp.float32)
    collected = []
    for position in range(window):
        carried, produced = advance(
            carried,
            step_size[:, position],
            inputs[:, position],
            entries[:, position],
            readouts[:, position],
            decay,
            skip_gain,
        )
        collected.append(produced)
    outputs = jnp.stack(collected, axis=1)
    outputs = outputs.reshape(slot_count, window, inner_here)
    gated = outputs * jax.nn.silu(gate_part.astype(jnp.float32))
    square_part = jnp.sum(gated * gated, axis=-1, keepdims=True)
    square_sum = lax.psum(square_part, "head")
    full_inner = inner_here * lax.axis_size("head")
    scaled = gated * lax.rsqrt(square_sum / full_inner + EPS) * gate_gain
    scaled = (
        jnp.where(valid[:, :, None], scaled, 0.0)
        .astype(jnp.bfloat16)
        .reshape(slot_count * window, inner_here)
    )
    mixer = lax.psum_scatter(
        jnp.dot(scaled, out_weight, preferred_element_type=jnp.float32).astype(jnp.bfloat16),
        "head",
        scatter_dimension=0,
        tiled=True,
    ).astype(jnp.float32)
    hidden_out = (rows_in + mixer).astype(jnp.bfloat16)
    return (hidden_out, carried.astype(jnp.bfloat16), edge_inner_out, edge_shared_out)


def solution(mesh):
    placed = (
        P(("req", "head"), None),
        P(),
        P(None, None, "head"),
        P(),
        P(None, "head"),
        P("head"),
        P(),
        P(),
        P("head"),
        P("head"),
        P("head"),
        P("head"),
        P("head", None),
        P("req", "head", None, None),
        P("req", None, "head"),
        P("req", None, None),
        P("req"),
        P(),
        P(),
        P(),
    )
    return jax.shard_map(
        local,
        mesh=mesh,
        in_specs=placed,
        out_specs=(
            P(("req", "head"), None),
            P("req", "head", None, None),
            P("req", None, "head"),
            P("req", None, None),
        ),
        check_vma=False,
    )
```

profile of v0, /device:TPU:2, one launch (start us, length us, event | category | flops | bytes accessed | tf_op | source)
XLA Modules:
  0.0 327.3 jit_solution(12424475779777113080)
XLA Ops:
  7.3 4.9 %copy.182 = bf16[32,6,64,128]{3,2,1,0:T(8,128)(2,1)} copy(bf16[32,6,64,128]{3,2,1,0:T(8,128)(2,1)} %param.39) | data formatting | bytes 6291456
  12.2 0.6 dynamic_slice.13
  13.5 1.5 constant_dynamic-slice_fusion.1
  15.0 1.3 bitcast_reduce_fusion
  18.1 24.2 %all_gather.15 = bf16[32,3,256]{2,1,0:T(4,128)(2,1)S(1)} all-gather(bf16[1,3,256]{2,1,0:T(4,128)(2,1)S(1)} %copy.132), channel_id=1, replica_groups=mesh['req'=32,'head'=8] {'req'}, dimensions={0}, use_global_device_ids=true | all-gather | bytes 50688 | tf_op jit(solution)/shard_map/all_gather | solution.py:111
  42.3 0.7 and_reduce_fusion
  43.0 0.6 dynamic-slice_select_fusion.2
  43.8 4.3 %scatter_custom_fusion = s32[1024]{0:T(1024)S(1)} fusion(s32[1024]{0:T(1024)S(1)} %compare_select_fusion.1, s32[1024]{0:T(1024)S(1)} %iota.23, s32[]{:T(128)} %constant.131.clone.1), kind=kCustom, calls=%fused_computation.125 | custom fusion | bytes 4100 | tf_op jit(solution)/shard_map/scatter | solution.py:52
  48.1 0.1 and_select_fusion.1
  48.3 0.2 convert_reduce_fusion.1
  48.5 0.7 broadcast_in_dim.159
  49.1 4.2 %scatter_fusion.2 = bf16[32,3,256]{2,1,0:T(4,128)(2,1)} fusion(bf16[32,3,256]{2,1,0:T(4,128)(2,1)} %broadcast_in_dim.159, s32[32]{0:T(128)S(1)} %compare_select_fusion.3, bf16[32,3,256]{2,1,0:T(4,128)(2,1)S(1)} %copy.100), kind=kCustom, calls=%fused_computation.6 | custom fusion | bytes 147584 | tf_op jit(solution)/shard_map/scatter | solution.py:48
  53.3 5.8 %all-to-all-start.2 = ((bf16[32,3,256]{2,1,0:T(4,128)(2,1)}), bf16[32,3,256]{2,1,0:T(4,128)(2,1)S(1)}, u32[]{:S(2)}, u32[]{:S(2)}) async-start(bf16[32,3,256]{2,1,0:T(4,128)(2,1)} %scatter_fusion.2), calls=%async_computation.2 | async-start | bytes 131072 | tf_op jit(solution)/shard_map/all_to_all | solution.py:134
  59.2 0.1 fusion.34
  59.4 28.8 %all_gather.13 = bf16[128,1536]{1,0:T(8,128)(2,1)S(1)} all-gather(bf16[16,1536]{1,0:T(8,128)(2,1)S(1)} %fusion.36), channel_id=1, replica_groups=mesh['req'=32,'head'=8] {'head'}, dimensions={0}, use_global_device_ids=true | all-gather | bytes 442368 | tf_op jit(solution)/shard_map/all_gather | solution.py:98
  88.2 0.4 convolution_convert_fusion.2
  88.6 0.1 copy.88
  88.8 2.1 copy.142
  91.0 0.5 convolution_convert_fusion.1
  91.6 0.1 constant_dynamic-slice_fusion.3
  91.7 0.1 copy.128
  91.8 24.0 %all_gather.14 = bf16[32,3,384]{2,1,0:T(4,128)(2,1)S(1)} all-gather(bf16[1,3,384]{2,1,0:T(4,128)(2,1)S(1)} %copy.130), channel_id=1, replica_groups=mesh['req'=32,'head'=8] {'req'}, dimensions={0}, use_global_device_ids=true | all-gather | bytes 76032 | tf_op jit(solution)/shard_map/all_gather | solution.py:110
  115.8 0.2 convert_reduce_fusion
  116.0 0.6 dynamic-slice_select_fusion.1
  116.6 0.1 fusion.49
  116.8 0.7 and_reduce_fusion.1
  117.6 0.7 broadcast_in_dim.158
  118.3 4.0 %scatter_fusion.1 = bf16[32,3,384]{2,1,0:T(4,128)(2,1)} fusion(bf16[32,3,384]{2,1,0:T(4,128)(2,1)} %broadcast_in_dim.158, s32[32]{0:T(128)S(1)} %compare_select_fusion.3, bf16[32,3,384]{2,1,0:T(4,128)(2,1)S(1)} %copy.95), kind=kCustom, calls=%fused_computation.5 | custom fusion | bytes 221312 | tf_op jit(solution)/shard_map/scatter | solution.py:48
  122.3 5.5 %all-to-all-start.1 = ((bf16[32,3,384]{2,1,0:T(4,128)(2,1)}), bf16[32,3,384]{2,1,0:T(4,128)(2,1)S(1)}, u32[]{:S(2)}, u32[]{:S(2)}) async-start(bf16[32,3,384]{2,1,0:T(4,128)(2,1)} %scatter_fusion.1), calls=%async_computation.1 | async-start | bytes 196608 | tf_op jit(solution)/shard_map/all_to_all | solution.py:127
  127.8 2.3 fusion.38
  130.0 2.5 broadcast_in_dim.83
  132.5 10.2 %scatter_fusion = bf16[32,6,64,128]{3,2,1,0:T(8,128)(2,1)} fusion(bf16[32,6,64,128]{3,2,1,0:T(8,128)(2,1)} %broadcast_in_dim.83, s32[32]{0:T(128)S(1)} %compare_select_fusion.3, bf16[32,6,64,128]{3,2,1,0:T(8,128)(2,1)} %fusion.38), kind=kCustom, calls=%fused_computation.4 | custom fusion | bytes 9437312 | tf_op jit(solution)/shard_map/scatter | solution.py:48
  142.7 7.6 %all-to-all-start = ((bf16[32,6,64,128]{3,2,1,0:T(8,128)(2,1)}), bf16[32,6,64,128]{3,2,1,0:T(8,128)(2,1)}, u32[]{:S(2)}, u32[]{:S(2)}) async-start(bf16[32,6,64,128]{3,2,1,0:T(8,128)(2,1)} %scatter_fusion), calls=%async_computation | async-start | bytes 6291456 | tf_op jit(solution)/shard_map/all_to_all | solution.py:120
  150.3 0.2 reduce-scatter.2.cloned.1.call-start
  150.6 0.1 copy.141
  150.7 0.1 copy.140
  150.7 0.1 copy.139
  150.8 0.1 copy.138
  150.9 0.1 copy.91
  151.0 0.1 copy.102
  151.2 0.1 copy.107
  151.5 0.6 gather_fusion.2
  152.1 0.3 fusion.45
  152.4 0.6 copy.116
  153.1 0.2 divide_multiply_fusion.1
  153.4 0.7 gather_fusion.1
  154.1 0.1 divide_multiply_fusion
  154.2 0.1 reshape.267
  154.4 0.7 fusion.41
  155.1 0.2 fusion.30
  155.3 34.7 %all-to-all-done = bf16[32,6,64,128]{3,2,1,0:T(8,128)(2,1)} async-done(((bf16[32,6,64,128]{3,2,1,0:T(8,128)(2,1)}), bf16[32,6,64,128]{3,2,1,0:T(8,128)(2,1)}, u32[]{:S(2)}, u32[]{:S(2)}) %all-to-all-start) | async-done | bytes 3145760 | tf_op jit(solution)/shard_map/all_to_all | solution.py:120
  190.0 4.5 %gather_fusion = bf16[32,6,64,128]{3,2,1,0:T(8,128)(2,1)} fusion(bf16[32,6,64,128]{3,2,1,0:T(8,128)(2,1)} %all-to-all-done, s32[1024]{0:T(1024)S(1)} %pad_clamp_fusion), kind=kCustom, calls=%fused_computation | custom fusion | bytes 6291584 | tf_op jit(solution)/shard_map/gather | solution.py:142
  194.5 16.5 %fusion = f32[32,1,6,64]{3,1,2,0:T(1,128)S(1)} fusion(bf16[32,6,64,128]{3,2,1,0:T(8,128)(2,1)} %gather_fusion, f32[32,128]{1,0:T(8,128)S(1)} %bitcast.123, f32[32,6,64]{2,1,0:T(8,128)S(1)} %get-tuple-element.136, f32[32,6]{1,0:T(8,128)S(1)} %copy.91, f32[32,4,256]{2,1,0:T(4,128)S(1)} %divide_multiply_fusion.1), kind=kOutput, calls=%fused_computation.11 | convolution fusion | flops 25165824 | bytes 3375104 | tf_op jit(solution)/shard_map/khpn,kn->khp/dot_general | solution.py:15
  211.1 16.0 %fusion.1 = f32[32,1,6,64]{3,1,2,0:T(1,128)S(1)} fusion(bf16[32,6,64,128]{3,2,1,0:T(8,128)(2,1)S(1)} %copy-done.1, f32[32,128]{1,0:T(8,128)S(1)} %bitcast.133, f32[32,6,64]{2,1,0:T(8,128)S(1)} %get-tuple-element.139, f32[32,6]{1,0:T(8,128)S(1)} %copy.102, f32[32,128]{1,0:T(8,128)S(1)} %bitcast.124, f32[32,6,64]{2,1,0:T(8,128)S(1)} %get-tuple-element.136, ...), kind=kOutput, calls=%fused_computation.12 | convolution fusion | flops 29884416 | bytes 3538944 | tf_op jit(solution)/shard_map/khpn,kn->khp/dot_general | solution.py:15
  227.1 19.6 %fusion.16 = f32[32,1,6,64]{3,1,2,0:T(1,128)S(1)} fusion(bf16[32,6,64,128]{3,2,1,0:T(8,128)(2,1)S(1)} %copy-done.1, f32[32,128]{1,0:T(8,128)S(1)} %bitcast.130, f32[32,6,64]{2,1,0:T(8,128)S(1)} %get-tuple-element.138, f32[32,6]{1,0:T(8,128)S(1)} %copy.105, f32[32,128]{1,0:T(8,128)S(1)} %bitcast.134, f32[32,6,64]{2,1,0:T(8,128)S(1)} %get-tuple-element.139, ...), kind=kOutput, calls=%fused_computation.28 | convolution fusion | flops 34603008 | bytes 3702784 | tf_op jit(solution)/shard_map/khpn,kn->khp/dot_general | solution.py:15
  246.8 21.4 %fusion.3 = f32[32,1,6,64]{3,1,2,0:T(1,128)S(1)} fusion(f32[32,128]{1,0:T(8,128)S(1)} %bitcast.128, f32[32,6,64]{2,1,0:T(8,128)S(1)} %get-tuple-element.137, f32[32,6]{1,0:T(8,128)S(1)} %copy.107, bf16[32,6,64,128]{3,2,1,0:T(8,128)(2,1)S(1)} %copy-done.1, f32[32,128]{1,0:T(8,128)S(1)} %bitcast.131, f32[32,6,64]{2,1,0:T(8,128)S(1)} %get-tuple-element.138, ...), kind=kOutput, calls=%fused_computation.14 | convolution fusion | flops 39321600 | bytes 3866624 | tf_op jit(solution)/shard_map/khpn,kn->khp/dot_general | solution.py:15
  268.1 0.1 bitcast_add_fusion.3
  268.6 0.1 multiply_reduce_fusion
  268.8 16.8 %psum.7 = f32[32,4,1]{0,1,2:T(4,128)S(1)} all-reduce(f32[32,4,1]{0,1,2:T(4,128)S(1)} %bitcast.137), channel_id=1, replica_groups=mesh['req'=32,'head'=8] {'head'}, use_global_device_ids=true, to_apply=%region_11.12 | all-reduce | flops 128 | bytes 1024 | tf_op jit(solution)/shard_map/psum | solution.py:185
  285.5 0.1 select_convert_fusion
  285.7 1.1 convolution_convert_fusion
  286.9 10.6 %fusion.2 = bf16[32,6,64,128]{3,2,1,0:T(8,128)(2,1)} fusion(f32[32,128]{1,0:T(8,128)S(1)} %bitcast.129, f32[32,6,64]{2,1,0:T(8,128)S(1)} %get-tuple-element.137, f32[32,6]{1,0:T(8,128)S(1)} %copy.107, f32[32,128]{1,0:T(8,128)S(1)} %bitcast.132, f32[32,6,64]{2,1,0:T(8,128)S(1)} %get-tuple-element.138, f32[32,6]{1,0:T(8,128)S(1)} %copy.105, ...), kind=kLoop, calls=%fused_computation.13 | loop fusion | flops 22020096 | bytes 6556672 | tf_op jit(solution)/shard_map/convert_element_type | solution.py:200
  297.5 21.5 %reduce-scatter.2.cloned.1.call-done = bf16[16,1536]{1,0:T(8,128)(2,1)} async-done(((bf16[128,1536]{1,0:T(8,128)(2,1)}), bf16[16,1536]{1,0:T(8,128)(2,1)}) %reduce-scatter.2.cloned.1.call-update) | async-done | bytes 49168 | tf_op jit(solution)/shard_map/reduce_scatter | solution.py:193
  319.0 1.4 fusion.37
  (94 shorter events, 1.8 us)
Async XLA Ops:
  7.2 278.6 %copy-start = (bf16[384,1536]{1,0:T(8,128)(2,1)S(1)}, bf16[384,1536]{1,0:T(8,128)(2,1)}, u32[]{:S(2)}) copy-start(bf16[384,1536]{1,0:T(8,128)(2,1)} %param.38) | copy-start | bytes 3538948
  7.2 35.1 %copy-start.18 = (s32[3]{0:T(128)S(1)}, s32[3]{0:T(128)}, u32[]{:S(2)}) copy-start(s32[3]{0:T(128)} %constant.151.clone.1) | copy-start | bytes 40
  7.2 52.0 %copy-start.3 = (bf16[16,1536]{1,0:T(8,128)(2,1)S(1)}, bf16[16,1536]{1,0:T(8,128)(2,1)}, u32[]{:S(2)}) copy-start(bf16[16,1536]{1,0:T(8,128)(2,1)} %param.26) | copy-start | bytes 147460
  7.2 52.1 %copy-start.6 = (f32[1536]{0:T(1024)S(1)}, f32[1536]{0:T(1024)}, u32[]{:S(2)}) copy-start(f32[1536]{0:T(1024)} %param.27) | copy-start | bytes 18436
  7.2 81.0 %copy-start.2 = (bf16[1536,304]{0,1:T(8,128)(2,1)S(1)}, bf16[1536,304]{0,1:T(8,128)(2,1)}, u32[]{:S(2)}) copy-start(bf16[1536,304]{0,1:T(8,128)(2,1)} %param.29) | copy-start | bytes 2801668
  7.2 5.0 %copy-start.4 = (bf16[32,3,384]{2,0,1:T(8,128)(2,1)S(1)}, bf16[32,3,384]{2,0,1:T(8,128)(2,1)}, u32[]{:S(2)}) copy-start(bf16[32,3,384]{2,0,1:T(8,128)(2,1)} %param.40) | copy-start | bytes 221188
  7.2 4.9 %copy-start.5 = (bf16[32,3,256]{2,0,1:T(8,128)(2,1)S(1)}, bf16[32,3,256]{2,0,1:T(8,128)(2,1)}, u32[]{:S(2)}) copy-start(bf16[32,3,256]{2,0,1:T(8,128)(2,1)} %param.41) | copy-start | bytes 147460
  7.2 5.0 %copy-start.19 = (s32[32]{0:T(128)S(1)}, s32[32]{0:T(128)}, u32[]{:S(2)}) copy-start(s32[32]{0:T(128)} %param.43) | copy-start | bytes 388
  7.3 7.8 %copy-start.16 = (s32[32]{0:T(128)S(1)}, s32[32]{0:T(128)}, u32[]{:S(2)}) copy-start(s32[32]{0:T(128)} %param.44) | copy-start | bytes 388
  7.3 36.5 %copy-start.8 = (s32[1024]{0:T(1024)S(1)}, s32[1024]{0:T(1024)}, u32[]{:S(2)}) copy-start(s32[1024]{0:T(1024)} %param.45) | copy-start | bytes 12292
  7.3 120.5 %all-gather.2.cloned.1.call-start = ((), (), s32[]{:S(2)}) async-start(), calls=%async_computation.4 | async-start | bytes 3244032 | tf_op jit(solution)/shard_map/all_gather | solution.py:109
  53.3 69.0 %all-to-all-start.2 = ((bf16[32,3,256]{2,1,0:T(4,128)(2,1)}), bf16[32,3,256]{2,1,0:T(4,128)(2,1)S(1)}, u32[]{:S(2)}, u32[]{:S(2)}) async-start(bf16[32,3,256]{2,1,0:T(4,128)(2,1)} %scatter_fusion.2), calls=%async_computation.2 | async-start | bytes 131072 | tf_op jit(solution)/shard_map/all_to_all | solution.py:134
  90.9 25.0 %copy-start.15 = (s32[32]{0:T(128)S(1)}, s32[32]{0:T(128)}, u32[]{:S(2)}) copy-start(s32[32]{0:T(128)} %param.42) | copy-start | bytes 388
  90.9 25.0 %copy-start.20 = (f32[6]{0:T(128)S(1)}, f32[6]{0:T(128)}, u32[]{:S(2)}) copy-start(f32[6]{0:T(128)} %param.35) | copy-start | bytes 76
  90.9 25.6 %copy-start.14 = (f32[6]{0:T(128)S(1)}, f32[6]{0:T(128)}, u32[]{:S(2)}) copy-start(f32[6]{0:T(128)} %param.34) | copy-start | bytes 76
  91.0 25.8 %copy-start.17 = (s32[4]{0:T(128)S(1)}, s32[4]{0:T(128)}, u32[]{:S(2)}) copy-start(s32[4]{0:T(128)} %constant.142.clone.1) | copy-start | bytes 52
  122.3 20.5 %all-to-all-start.1 = ((bf16[32,3,384]{2,1,0:T(4,128)(2,1)}), bf16[32,3,384]{2,1,0:T(4,128)(2,1)S(1)}, u32[]{:S(2)}, u32[]{:S(2)}) async-start(bf16[32,3,384]{2,1,0:T(4,128)(2,1)} %scatter_fusion.1), calls=%async_computation.1 | async-start | bytes 196608 | tf_op jit(solution)/shard_map/all_to_all | solution.py:127
  142.7 8.6 %copy-start.7 = (f32[4,384]{1,0:T(4,128)S(1)}, f32[4,384]{1,0:T(4,128)}, u32[]{:S(2)}) copy-start(f32[4,384]{1,0:T(4,128)} %param.30) | copy-start | bytes 18436
  142.7 8.6 %copy-start.9 = (f32[4,256]{1,0:T(4,128)S(1)}, f32[4,256]{1,0:T(4,128)}, u32[]{:S(2)}) copy-start(f32[4,256]{1,0:T(4,128)} %param.32) | copy-start | bytes 12292
  142.7 10.4 %copy-start.12 = (f32[256]{0:T(256)S(1)}, f32[256]{0:T(256)}, u32[]{:S(2)}) copy-start(f32[256]{0:T(256)} %param.33) | copy-start | bytes 3076
  142.7 47.3 %all-to-all-start = ((bf16[32,6,64,128]{3,2,1,0:T(8,128)(2,1)}), bf16[32,6,64,128]{3,2,1,0:T(8,128)(2,1)}, u32[]{:S(2)}, u32[]{:S(2)}) async-start(bf16[32,6,64,128]{3,2,1,0:T(8,128)(2,1)} %scatter_fusion), calls=%async_computation | async-start | bytes 6291456 | tf_op jit(solution)/shard_map/all_to_all | solution.py:120
  150.3 3.8 %copy-start.10 = (f32[384]{0:T(512)S(1)}, f32[384]{0:T(512)}, u32[]{:S(2)}) copy-start(f32[384]{0:T(512)} %param.31) | copy-start | bytes 4612
  150.3 168.7 %reduce-scatter.2.cloned.1.call-start = ((), (), s32[]{:S(2)}) async-start(), calls=%async_computation.5 | async-start | bytes 442368 | tf_op jit(solution)/shard_map/reduce_scatter | solution.py:193
  194.5 16.6 %copy-start.1 = (bf16[32,6,64,128]{3,2,1,0:T(8,128)(2,1)S(1)}, bf16[32,6,64,128]{3,2,1,0:T(8,128)(2,1)}, u32[]{:S(2)}) copy-start(bf16[32,6,64,128]{3,2,1,0:T(8,128)(2,1)} %gather_fusion) | copy-start | bytes 9437188
  246.7 21.4 %copy-start.13 = (f32[6]{0:T(128)S(1)}, f32[6]{0:T(128)}, u32[]{:S(2)}) copy-start(f32[6]{0:T(128)} %param.36) | copy-start | bytes 76
  246.7 38.8 %copy-start.11 = (f32[384]{0:T(512)S(1)}, f32[384]{0:T(512)}, u32[]{:S(2)}) copy-start(f32[384]{0:T(512)} %param.37) | copy-start | bytes 4612
Sparse Core Ops, SparseCore 0:
  15.2 53.5 all-gather.1
  287.0 31.9 reduce-scatter.1
where the time goes:
time: 328 us; the launch traced here: 327 us
  blocking collectives  93.7 us (29%)
  matrix products  75.5 us (23%)
  waiting for transfers between devices  56.3 us (17%)
  local copies, waits for them, and re-layouts  44.3 us (14%)
  other arithmetic  21.2 us (6%)
  starting transfers between devices  19.1 us (6%)
  between operations  17.1 us (5%)
    dot_general x4, matrix products, advance(): jnp.einsum('khpn,kn->khp', carried, readout_now, precision=lax.Precision....  73.5 us
    all_to_all x1, waiting for transfers between devices, local(): lax.all_to_all(pack_pages(sectioned_states, send_rows, buffer_rows), 'req...  34.7 us
    all_gather x1, blocking collectives, local(): piece_rows = lax.all_gather(normed, 'head', axis=0, tiled=True)  28.8 us
    all_gather x1, blocking collectives, local(): lax.all_gather(edge_shared[local_ids], 'req', axis=0, tiled=True)  24.2 us
    all_gather x1, blocking collectives, local(): lax.all_gather(edge_inner[local_ids], 'req', axis=0, tiled=True)  24 us
    reduce_scatter x1, waiting for transfers between devices, local(): lax.psum_scatter(jnp.dot(scaled, out_weight, preferred_element_type=jnp.f...  21.5 us
    scatter x3, local copies, waits for them, and re-layouts, pack_pages(): return empty.at[send_rows].set(member)  18.4 us
    psum x1, blocking collectives, local(): square_sum = lax.psum(square_part, 'head')  16.8 us
  transfers between devices with their start and end apart: 5, of which 2 were waited for; matrix products, arithmetic and copies ran while one was open for 16% of the time, Pallas kernels for 0%

commit v1 on v0

--- a/solution.py
+++ b/solution.py
@@ -95,7 +95,23 @@
         rows_in * lax.rsqrt(jnp.mean(rows_in * rows_in, axis=-1, keepdims=True) + EPS) * pre_gain
     ).astype(jnp.bfloat16)
     inner_flat = inner_weight.reshape(inner_weight.shape[0], 2 * inner_here)
-    piece_rows = lax.all_gather(normed, "head", axis=0, tiled=True)
+    ways, here, step = (lax.axis_size("head"), lax.axis_index("head"), normed.shape[0])
+    dims = [n * ways if d == 0 else n for d, n in enumerate(normed.shape)]
+    full = lax.dynamic_update_slice_in_dim(
+        jnp.zeros(dims, normed.dtype), normed, here * step, axis=0
+    )
+    going_up = going_down = normed
+    for far in range(1, ways // 2 + 1):
+        going_up = lax.ppermute(going_up, "head", [(d, (d + 1) % ways) for d in range(ways)])
+        full = lax.dynamic_update_slice_in_dim(full, going_up, (here - far) % ways * step, axis=0)
+        if 2 * far < ways:
+            going_down = lax.ppermute(
+                going_down, "head", [(d, (d - 1) % ways) for d in range(ways)]
+            )
+            full = lax.dynamic_update_slice_in_dim(
+                full, going_down, (here + far) % ways * step, axis=0
+            )
+    piece_rows = full
     inner_rows = jnp.dot(piece_rows, inner_flat, preferred_element_type=jnp.float32).astype(
         jnp.bfloat16
     )

time: 328 us -> 341 us (1.040)
  blocking collectives: 93.7 us -> 62.5 us
  local copies, waits for them, and re-layouts: 44.3 us -> 60.6 us
  starting transfers between devices: 19.1 us -> 31.4 us
  waiting for transfers between devices: 56.3 us -> 64.2 us
  matrix products: 75.5 us -> 79.2 us
    all_gather x1 -> x0, blocking collectives: 28.8 us -> none  [local(): piece_rows = lax.all_gather(normed, 'head', axis=0, tiled=True)]
    ppermute x0 -> x7, starting transfers between devices: none -> 12.3 us  [the longest x3 10.4 us: local(): lax.ppermute(going_down, 'head', [(d, (d - 1) % ways) for d in range(ways)])]
    dynamic_update_slice x0 -> x7, local copies, waits for them, and re-layouts: none -> 7.55 us  [the longest x4 4.09 us: local(): lax.dynamic_update_slice_in_dim(full, going_up, (here - far) % ways * ste...]
    ppermute x0 -> x7, waiting for transfers between devices: none -> 4.06 us  [the longest x4 4.05 us: local(): lax.ppermute(going_up, 'head', [(d, (d + 1) % ways) for d in range(ways)])]
    unnamed x52 -> x86, local copies, waits for them, and re-layouts: 7.97 us -> 9.44 us
  transfers between devices with their start and end apart: 5 -> 12, of which waited for: 2 -> 3; matrix products, arithmetic and copies ran while one was open for 16% -> 18% of each run, Pallas kernels for 0% -> 0%
where the time goes in v1:
time: 341 us; the launch traced here: 340 us
  matrix products  79.2 us (23%)
  waiting for transfers between devices  64.2 us (19%)
  blocking collectives  62.5 us (18%)
  local copies, waits for them, and re-layouts  60.6 us (18%)
  starting transfers between devices  31.4 us (9%)
  other arithmetic  24.5 us (7%)
  between operations  17.4 us (5%)
    dot_general x4, matrix products, advance(): jnp.einsum('khpn,kn->khp', carried, readout_now, precision=lax.Precision....  73.5 us
    all_to_all x1, waiting for transfers between devices, local(): lax.all_to_all(pack_pages(sectioned_states, send_rows, buffer_rows), 'req...  35.6 us
    reduce_scatter x1, waiting for transfers between devices, local(): lax.psum_scatter(jnp.dot(scaled, out_weight, preferred_element_type=jnp.f...  24.5 us
    all_gather x1, blocking collectives, local(): lax.all_gather(edge_shared[local_ids], 'req', axis=0, tiled=True)  24.2 us
    all_gather x1, blocking collectives, local(): lax.all_gather(edge_inner[local_ids], 'req', axis=0, tiled=True)  24.2 us
    scatter x3, local copies, waits for them, and re-layouts, pack_pages(): return empty.at[send_rows].set(member)  18.8 us
    psum x1, blocking collectives, local(): square_sum = lax.psum(square_part, 'head')  14.2 us
    convert_element_type x1, other arithmetic, local(): carried.astype(jnp.bfloat16)  10.6 us
  transfers between devices with their start and end apart: 12, of which 3 were waited for; matrix products, arithmetic and copies ran while one was open for 18% of the time, Pallas kernels for 0%

profile of v1, /device:TPU:2, one launch (start us, length us, event | category | flops | bytes accessed | tf_op | source)
XLA Modules:
  0.0 339.7 jit_solution(14849244150150507839)
XLA Ops:
  7.4 4.7 %copy.190 = bf16[32,6,64,128]{3,2,1,0:T(8,128)(2,1)} copy(bf16[32,6,64,128]{3,2,1,0:T(8,128)(2,1)} %param.39) | data formatting | bytes 6291456
  12.2 0.6 dynamic_slice.13
  13.4 1.5 constant_dynamic-slice_fusion.1
  15.1 0.8 broadcast_in_dim.161
  15.9 0.7 constant_dynamic-update-slice_fusion.7
  16.6 1.9 collective-permute-start
  18.5 3.9 %collective-permute-start.1 = (bf16[16,1536]{1,0:T(8,128)(2,1)}, bf16[16,1536]{1,0:T(8,128)(2,1)}, u32[]{:S(2)}, u32[]{:S(2)}) collective-permute-start(bf16[16,1536]{1,0:T(8,128)(2,1)} %get-tuple-element.133), channel_id=1, source_target_pairs={{0,7},{1,0},{2,1},{3,2},{4,3},{5,4},{6,5},{7,6},{8,15},{9,8},{10,9... | collective-permute-start | bytes 147464 | tf_op jit(solution)/shard_map/ppermute | solution.py:108
  22.5 1.4 bitcast_reduce_fusion
  25.8 24.2 %all_gather.11 = bf16[32,3,256]{2,1,0:T(4,128)(2,1)S(1)} all-gather(bf16[1,3,256]{2,1,0:T(4,128)(2,1)S(1)} %copy.132), channel_id=1, replica_groups=mesh['req'=32,'head'=8] {'req'}, dimensions={0}, use_global_device_ids=true | all-gather | bytes 50688 | tf_op jit(solution)/shard_map/all_gather | solution.py:127
  49.9 0.8 and_reduce_fusion
  50.7 0.7 fusion.58
  51.6 4.3 %scatter_custom_fusion = s32[1024]{0:T(1024)S(1)} fusion(s32[1024]{0:T(1024)S(1)} %compare_select_fusion.1, s32[1024]{0:T(1024)S(1)} %iota.23, s32[]{:T(128)} %constant.176.clone.1), kind=kCustom, calls=%fused_computation.139 | custom fusion | bytes 4100 | tf_op jit(solution)/shard_map/scatter | solution.py:52
  56.1 0.2 convert_reduce_fusion.1
  56.3 0.6 broadcast_in_dim.163
  56.9 4.2 %scatter_fusion.2 = bf16[32,3,256]{2,1,0:T(4,128)(2,1)} fusion(bf16[32,3,256]{2,1,0:T(4,128)(2,1)} %broadcast_in_dim.163, s32[32]{0:T(128)S(1)} %compare_select_fusion.3, bf16[32,3,256]{2,1,0:T(4,128)(2,1)S(1)} %copy.100), kind=kCustom, calls=%fused_computation.6 | custom fusion | bytes 147584 | tf_op jit(solution)/shard_map/scatter | solution.py:48
  61.1 5.9 %all-to-all-start.2 = ((bf16[32,3,256]{2,1,0:T(4,128)(2,1)}), bf16[32,3,256]{2,1,0:T(4,128)(2,1)}, u32[]{:S(2)}, u32[]{:S(2)}) async-start(bf16[32,3,256]{2,1,0:T(4,128)(2,1)} %scatter_fusion.2), calls=%async_computation.2 | async-start | bytes 131072 | tf_op jit(solution)/shard_map/all_to_all | solution.py:150
  67.1 24.2 %all_gather.10 = bf16[32,3,384]{2,1,0:T(4,128)(2,1)S(1)} all-gather(bf16[1,3,384]{2,1,0:T(4,128)(2,1)S(1)} %copy.130), channel_id=1, replica_groups=mesh['req'=32,'head'=8] {'req'}, dimensions={0}, use_global_device_ids=true | all-gather | bytes 76032 | tf_op jit(solution)/shard_map/all_gather | solution.py:126
  91.2 0.7 and_reduce_fusion.1
  92.2 0.6 iota_compare_fusion.1
  92.8 0.5 exponential_negate_fusion
  93.3 0.6 broadcast_compare_fusion.2
  93.9 0.7 fusion.57
  94.6 0.6 fusion.67
  95.2 0.6 pad_clamp_fusion
  95.9 0.7 copy.95
  96.6 2.1 copy.142
  98.7 0.6 broadcast_in_dim.162
  99.4 4.4 %scatter_fusion.1 = bf16[32,3,384]{2,1,0:T(4,128)(2,1)} fusion(bf16[32,3,384]{2,1,0:T(4,128)(2,1)} %broadcast_in_dim.162, s32[32]{0:T(128)} %copy-done.14, bf16[32,3,384]{2,1,0:T(4,128)(2,1)} %copy.95), kind=kCustom, calls=%fused_computation.5 | custom fusion | bytes 221312 | tf_op jit(solution)/shard_map/scatter | solution.py:48
  103.8 5.5 %all-to-all-start.1 = ((bf16[32,3,384]{2,1,0:T(4,128)(2,1)}), bf16[32,3,384]{2,1,0:T(4,128)(2,1)}, u32[]{:S(2)}, u32[]{:S(2)}) async-start(bf16[32,3,384]{2,1,0:T(4,128)(2,1)} %scatter_fusion.1), calls=%async_computation.1 | async-start | bytes 196608 | tf_op jit(solution)/shard_map/all_to_all | solution.py:143
  109.3 2.2 gather_fusion.2
  111.5 3.2 collective-permute-start.3
  114.8 1.4 constant_dynamic-update-slice_fusion.6
  116.2 1.4 constant_dynamic-update-slice_fusion.5
  117.6 2.3 gather_fusion.1
  119.9 1.5 copy_dynamic-update-slice_fusion.1
  121.5 3.2 collective-permute-start.5
  124.7 1.4 constant_dynamic-update-slice_fusion.4
  126.1 1.4 constant_dynamic-update-slice_fusion.3
  127.5 0.6 constant_dynamic-update-slice_fusion.2
  128.2 0.6 constant_dynamic-update-slice_fusion.1
  128.8 4.0 %collective-permute-done.6 = bf16[16,1536]{1,0:T(8,128)(2,1)S(1)} collective-permute-done((bf16[16,1536]{1,0:T(8,128)(2,1)S(1)}, bf16[16,1536]{1,0:T(8,128)(2,1)S(1)}, u32[]{:S(2)}, u32[]{:S(2)}) %collective-permute-start.6) | collective-permute-done | bytes 49184 | tf_op jit(solution)/shard_map/ppermute | solution.py:105
  132.8 0.6 constant_dynamic-update-slice_fusion
  133.5 2.3 convolution_convert_fusion.2
  135.8 1.6 copy.88
  137.4 2.2 convolution_convert_fusion.1
  139.6 2.2 fusion.38
  141.8 2.5 broadcast_in_dim.85
  144.3 10.2 %scatter_fusion = bf16[32,6,64,128]{3,2,1,0:T(8,128)(2,1)} fusion(bf16[32,6,64,128]{3,2,1,0:T(8,128)(2,1)} %broadcast_in_dim.85, s32[32]{0:T(128)S(1)} %copy-done.15, bf16[32,6,64,128]{3,2,1,0:T(8,128)(2,1)} %fusion.38), kind=kCustom, calls=%fused_computation.4 | custom fusion | bytes 9437312 | tf_op jit(solution)/shard_map/scatter | solution.py:48
  154.6 7.6 %all-to-all-start = ((bf16[32,6,64,128]{3,2,1,0:T(8,128)(2,1)}), bf16[32,6,64,128]{3,2,1,0:T(8,128)(2,1)}, u32[]{:S(2)}, u32[]{:S(2)}) async-start(bf16[32,6,64,128]{3,2,1,0:T(8,128)(2,1)} %scatter_fusion), calls=%async_computation | async-start | bytes 6291456 | tf_op jit(solution)/shard_map/all_to_all | solution.py:136
  163.6 0.3 fusion.45
  163.9 0.6 copy.116
  165.4 0.7 fusion.41
  166.1 0.2 fusion.30
  166.3 35.6 %all-to-all-done = bf16[32,6,64,128]{3,2,1,0:T(8,128)(2,1)} async-done(((bf16[32,6,64,128]{3,2,1,0:T(8,128)(2,1)}), bf16[32,6,64,128]{3,2,1,0:T(8,128)(2,1)}, u32[]{:S(2)}, u32[]{:S(2)}) %all-to-all-start) | async-done | bytes 3145760 | tf_op jit(solution)/shard_map/all_to_all | solution.py:136
  201.9 4.6 %gather_fusion = bf16[32,6,64,128]{3,2,1,0:T(8,128)(2,1)} fusion(bf16[32,6,64,128]{3,2,1,0:T(8,128)(2,1)} %all-to-all-done, s32[1024]{0:T(1024)} %pad_clamp_fusion), kind=kCustom, calls=%fused_computation | custom fusion | bytes 6291584 | tf_op jit(solution)/shard_map/gather | solution.py:158
  206.5 16.5 %fusion = f32[32,1,6,64]{3,1,2,0:T(1,128)S(1)} fusion(bf16[32,6,64,128]{3,2,1,0:T(8,128)(2,1)} %gather_fusion, f32[32,128]{1,0:T(8,128)S(1)} %bitcast.123, f32[32,6,64]{2,1,0:T(8,128)S(1)} %get-tuple-element.138, f32[32,6]{1,0:T(8,128)S(1)} %copy.91, f32[32,4,256]{2,1,0:T(4,128)S(1)} %divide_multiply_fusion.1), kind=kOutput, calls=%fused_computation.11 | convolution fusion | flops 25165824 | bytes 3375104 | tf_op jit(solution)/shard_map/khpn,kn->khp/dot_general | solution.py:15
  223.1 16.0 %fusion.1 = f32[32,1,6,64]{3,1,2,0:T(1,128)S(1)} fusion(bf16[32,6,64,128]{3,2,1,0:T(8,128)(2,1)S(1)} %copy-done.1, f32[32,128]{1,0:T(8,128)S(1)} %bitcast.133, f32[32,6,64]{2,1,0:T(8,128)S(1)} %get-tuple-element.141, f32[32,6]{1,0:T(8,128)S(1)} %copy.102, f32[32,128]{1,0:T(8,128)S(1)} %bitcast.124, f32[32,6,64]{2,1,0:T(8,128)S(1)} %get-tuple-element.138, ...), kind=kOutput, calls=%fused_computation.12 | convolution fusion | flops 29884416 | bytes 3538944 | tf_op jit(solution)/shard_map/khpn,kn->khp/dot_general | solution.py:15
  239.1 19.6 %fusion.16 = f32[32,1,6,64]{3,1,2,0:T(1,128)S(1)} fusion(bf16[32,6,64,128]{3,2,1,0:T(8,128)(2,1)S(1)} %copy-done.1, f32[32,128]{1,0:T(8,128)S(1)} %bitcast.130, f32[32,6,64]{2,1,0:T(8,128)S(1)} %get-tuple-element.140, f32[32,6]{1,0:T(8,128)S(1)} %copy.105, f32[32,128]{1,0:T(8,128)S(1)} %bitcast.134, f32[32,6,64]{2,1,0:T(8,128)S(1)} %get-tuple-element.141, ...), kind=kOutput, calls=%fused_computation.28 | convolution fusion | flops 34603008 | bytes 3702784 | tf_op jit(solution)/shard_map/khpn,kn->khp/dot_general | solution.py:15
  258.7 21.4 %fusion.3 = f32[32,1,6,64]{3,1,2,0:T(1,128)S(1)} fusion(f32[32,128]{1,0:T(8,128)S(1)} %bitcast.128, f32[32,6,64]{2,1,0:T(8,128)S(1)} %get-tuple-element.139, f32[32,6]{1,0:T(8,128)S(1)} %copy.107, bf16[32,6,64,128]{3,2,1,0:T(8,128)(2,1)S(1)} %copy-done.1, f32[32,128]{1,0:T(8,128)S(1)} %bitcast.131, f32[32,6,64]{2,1,0:T(8,128)S(1)} %get-tuple-element.140, ...), kind=kOutput, calls=%fused_computation.14 | convolution fusion | flops 39321600 | bytes 3866624 | tf_op jit(solution)/shard_map/khpn,kn->khp/dot_general | solution.py:15
  280.7 14.2 %psum.7 = f32[32,4,1]{0,1,2:T(4,128)S(1)} all-reduce(f32[32,4,1]{0,1,2:T(4,128)S(1)} %bitcast.137), channel_id=1, replica_groups=mesh['req'=32,'head'=8] {'head'}, use_global_device_ids=true, to_apply=%region_11.12 | all-reduce | flops 128 | bytes 1024 | tf_op jit(solution)/shard_map/psum | solution.py:201
  295.1 1.1 convolution_convert_fusion
  296.3 10.6 %fusion.2 = bf16[32,6,64,128]{3,2,1,0:T(8,128)(2,1)} fusion(f32[32,128]{1,0:T(8,128)S(1)} %bitcast.129, f32[32,6,64]{2,1,0:T(8,128)S(1)} %get-tuple-element.139, f32[32,6]{1,0:T(8,128)S(1)} %copy.107, f32[32,128]{1,0:T(8,128)S(1)} %bitcast.132, f32[32,6,64]{2,1,0:T(8,128)S(1)} %get-tuple-element.140, f32[32,6]{1,0:T(8,128)S(1)} %copy.105, ...), kind=kLoop, calls=%fused_computation.13 | loop fusion | flops 22020096 | bytes 6556672 | tf_op jit(solution)/shard_map/convert_element_type | solution.py:216
  306.9 24.5 %reduce-scatter.2.cloned.1.call-done = bf16[16,1536]{1,0:T(8,128)(2,1)} async-done(((bf16[128,1536]{1,0:T(8,128)(2,1)}), bf16[16,1536]{1,0:T(8,128)(2,1)}) %reduce-scatter.2.cloned.1.call-update) | async-done | bytes 49168 | tf_op jit(solution)/shard_map/reduce_scatter | solution.py:209
  331.5 1.4 fusion.37
  (149 shorter events, 3.8 us)
Async XLA Ops:
  7.2 287.9 %copy-start = (bf16[384,1536]{1,0:T(8,128)(2,1)S(1)}, bf16[384,1536]{1,0:T(8,128)(2,1)}, u32[]{:S(2)}) copy-start(bf16[384,1536]{1,0:T(8,128)(2,1)} %param.38) | copy-start | bytes 3538948
  7.2 42.8 %copy-start.35 = (s32[3]{0:T(128)S(1)}, s32[3]{0:T(128)}, u32[]{:S(2)}) copy-start(s32[3]{0:T(128)} %constant.205.clone.1) | copy-start | bytes 40
  7.2 84.0 %copy-start.34 = (s32[4]{0:T(128)S(1)}, s32[4]{0:T(128)}, u32[]{:S(2)}) copy-start(s32[4]{0:T(128)} %constant.187.clone.1) | copy-start | bytes 52
  7.2 7.8 %copy-start.6 = (bf16[16,1536]{1,0:T(8,128)(2,1)S(1)}, bf16[16,1536]{1,0:T(8,128)(2,1)}, u32[]{:S(2)}) copy-start(bf16[16,1536]{1,0:T(8,128)(2,1)} %param.26) | copy-start | bytes 147460
  7.2 8.7 %copy-start.11 = (f32[1536]{0:T(1024)S(1)}, f32[1536]{0:T(1024)}, u32[]{:S(2)}) copy-start(f32[1536]{0:T(1024)} %param.27) | copy-start | bytes 18436
  7.2 84.7 %copy-start.12 = (f32[4,384]{1,0:T(4,128)S(1)}, f32[4,384]{1,0:T(4,128)}, u32[]{:S(2)}) copy-start(f32[4,384]{1,0:T(4,128)} %param.30) | copy-start | bytes 18436
  7.2 87.4 %copy-start.24 = (f32[4,256]{1,0:T(4,128)S(1)}, f32[4,256]{1,0:T(4,128)}, u32[]{:S(2)}) copy-start(f32[4,256]{1,0:T(4,128)} %param.32) | copy-start | bytes 12292
  7.3 85.5 %copy-start.37 = (f32[6]{0:T(128)S(1)}, f32[6]{0:T(128)}, u32[]{:S(2)}) copy-start(f32[6]{0:T(128)} %param.35) | copy-start | bytes 76
  7.3 4.9 %copy-start.9 = (bf16[32,3,384]{2,0,1:T(8,128)(2,1)S(1)}, bf16[32,3,384]{2,0,1:T(8,128)(2,1)}, u32[]{:S(2)}) copy-start(bf16[32,3,384]{2,0,1:T(8,128)(2,1)} %param.40) | copy-start | bytes 221188
  7.3 4.8 %copy-start.10 = (bf16[32,3,256]{2,0,1:T(8,128)(2,1)S(1)}, bf16[32,3,256]{2,0,1:T(8,128)(2,1)}, u32[]{:S(2)}) copy-start(bf16[32,3,256]{2,0,1:T(8,128)(2,1)} %param.41) | copy-start | bytes 147460
  7.3 84.9 %copy-start.31 = (s32[32]{0:T(128)S(1)}, s32[32]{0:T(128)}, u32[]{:S(2)}) copy-start(s32[32]{0:T(128)} %param.42) | copy-start | bytes 388
  7.3 4.9 %copy-start.36 = (s32[32]{0:T(128)S(1)}, s32[32]{0:T(128)}, u32[]{:S(2)}) copy-start(s32[32]{0:T(128)} %param.43) | copy-start | bytes 388
  7.3 15.2 %copy-start.33 = (s32[32]{0:T(128)S(1)}, s32[32]{0:T(128)}, u32[]{:S(2)}) copy-start(s32[32]{0:T(128)} %param.44) | copy-start | bytes 388
  7.3 44.2 %copy-start.13 = (s32[1024]{0:T(1024)S(1)}, s32[1024]{0:T(1024)}, u32[]{:S(2)}) copy-start(s32[1024]{0:T(1024)} %param.45) | copy-start | bytes 12292
  7.3 132.3 %all-gather.2.cloned.1.call-start = ((), (), s32[]{:S(2)}) async-start(), calls=%async_computation.4 | async-start | bytes 3244032 | tf_op jit(solution)/shard_map/all_gather | solution.py:125
  16.6 94.9 %collective-permute-start = (bf16[16,1536]{1,0:T(8,128)(2,1)}, bf16[16,1536]{1,0:T(8,128)(2,1)}, u32[]{:S(2)}, u32[]{:S(2)}) collective-permute-start(bf16[16,1536]{1,0:T(8,128)(2,1)} %get-tuple-element.133), channel_id=1, source_target_pairs={{0,1},{1,2},{2,3},{3,4},{4,5},{5,6},{6,7},{7,0},{8,9},{9,10},{10,1... | collective-permute-start | bytes 147464 | tf_op jit(solution)/shard_map/ppermute | solution.py:105
  18.5 93.0 %collective-permute-start.1 = (bf16[16,1536]{1,0:T(8,128)(2,1)}, bf16[16,1536]{1,0:T(8,128)(2,1)}, u32[]{:S(2)}, u32[]{:S(2)}) collective-permute-start(bf16[16,1536]{1,0:T(8,128)(2,1)} %get-tuple-element.133), channel_id=1, source_target_pairs={{0,7},{1,0},{2,1},{3,2},{4,3},{5,4},{6,5},{7,6},{8,15},{9,8},{10,9... | collective-permute-start | bytes 147464 | tf_op jit(solution)/shard_map/ppermute | solution.py:108
  56.2 39.6 %copy-start.14 = (s32[32]{0:T(128)}, s32[32]{0:T(128)S(1)}, u32[]{:S(2)}) copy-start(s32[32]{0:T(128)S(1)} %compare_select_fusion.3) | copy-start | bytes 388
  61.1 42.6 %all-to-all-start.2 = ((bf16[32,3,256]{2,1,0:T(4,128)(2,1)}), bf16[32,3,256]{2,1,0:T(4,128)(2,1)}, u32[]{:S(2)}, u32[]{:S(2)}) async-start(bf16[32,3,256]{2,1,0:T(4,128)(2,1)} %scatter_fusion.2), calls=%async_computation.2 | async-start | bytes 131072 | tf_op jit(solution)/shard_map/all_to_all | solution.py:150
  103.8 13.8 %all-to-all-start.1 = ((bf16[32,3,384]{2,1,0:T(4,128)(2,1)}), bf16[32,3,384]{2,1,0:T(4,128)(2,1)}, u32[]{:S(2)}, u32[]{:S(2)}) async-start(bf16[32,3,384]{2,1,0:T(4,128)(2,1)} %scatter_fusion.1), calls=%async_computation.1 | async-start | bytes 196608 | tf_op jit(solution)/shard_map/all_to_all | solution.py:143
  111.5 9.9 %collective-permute-start.2 = (bf16[16,1536]{1,0:T(8,128)(2,1)}, bf16[16,1536]{1,0:T(8,128)(2,1)}, u32[]{:S(2)}, u32[]{:S(2)}) collective-permute-start(bf16[16,1536]{1,0:T(8,128)(2,1)} %collective-permute-done), channel_id=1, source_target_pairs={{0,1},{1,2},{2,3},{3,4},{4,5},{5,6},{6,7},{7,0},{8,9},{9,10},{10,1... | collective-permute-start | bytes 147464 | tf_op jit(solution)/shard_map/ppermute | solution.py:105
  111.5 9.9 %collective-permute-start.3 = (bf16[16,1536]{1,0:T(8,128)(2,1)}, bf16[16,1536]{1,0:T(8,128)(2,1)}, u32[]{:S(2)}, u32[]{:S(2)}) collective-permute-start(bf16[16,1536]{1,0:T(8,128)(2,1)} %collective-permute-done.1), channel_id=1, source_target_pairs={{0,7},{1,0},{2,1},{3,2},{4,3},{5,4},{6,5},{7,6},{8,15},{9,8},{10,9... | collective-permute-start | bytes 147464 | tf_op jit(solution)/shard_map/ppermute | solution.py:108
  121.4 6.1 %collective-permute-start.4 = (bf16[16,1536]{1,0:T(8,128)(2,1)}, bf16[16,1536]{1,0:T(8,128)(2,1)S(1)}, u32[]{:S(2)}, u32[]{:S(2)}) collective-permute-start(bf16[16,1536]{1,0:T(8,128)(2,1)} %collective-permute-done.2), channel_id=1, source_target_pairs={{0,1},{1,2},{2,3},{3,4},{4,5},{5,6},{6,7},{7,0},{8,9},{9,10},{10,1... | collective-permute-start | bytes 147464 | tf_op jit(solution)/shard_map/ppermute | solution.py:105
  121.5 6.7 %collective-permute-start.5 = (bf16[16,1536]{1,0:T(8,128)(2,1)}, bf16[16,1536]{1,0:T(8,128)(2,1)S(1)}, u32[]{:S(2)}, u32[]{:S(2)}) collective-permute-start(bf16[16,1536]{1,0:T(8,128)(2,1)} %collective-permute-done.3), channel_id=1, source_target_pairs={{0,7},{1,0},{2,1},{3,2},{4,3},{5,4},{6,5},{7,6},{8,15},{9,8},{10,9... | collective-permute-start | bytes 147464 | tf_op jit(solution)/shard_map/ppermute | solution.py:108
  127.5 5.3 %collective-permute-start.6 = (bf16[16,1536]{1,0:T(8,128)(2,1)S(1)}, bf16[16,1536]{1,0:T(8,128)(2,1)S(1)}, u32[]{:S(2)}, u32[]{:S(2)}) collective-permute-start(bf16[16,1536]{1,0:T(8,128)(2,1)S(1)} %collective-permute-done.4), channel_id=1, source_target_pairs={{0,1},{1,2},{2,3},{3,4},{4,5},{5,6},{6,7},{7,0},{8,9},{9,10},{10,1... | collective-permute-start | bytes 147464 | tf_op jit(solution)/shard_map/ppermute | solution.py:105
  139.6 4.7 %copy-start.15 = (s32[32]{0:T(128)S(1)}, s32[32]{0:T(128)}, u32[]{:S(2)}) copy-start(s32[32]{0:T(128)} %copy-done.14) | copy-start | bytes 388
  154.5 7.8 %copy-start.4 = (bf16[128,768]{1,0:T(8,128)(2,1)S(1)}, bf16[128,768]{1,0:T(8,128)(2,1)}, u32[]{:S(2)}) copy-start(bf16[128,768]{1,0:T(8,128)(2,1)} %convolution_convert_fusion.1) | copy-start | bytes 589828
  154.5 7.8 %copy-start.8 = (bf16[128,304]{1,0:T(8,128)(2,1)S(1)}, bf16[128,304]{1,0:T(8,128)(2,1)}, u32[]{:S(2)}) copy-start(bf16[128,304]{1,0:T(8,128)(2,1)} %copy.88) | copy-start | bytes 233476
  154.5 8.2 %copy-start.27 = (pred[32,4]{0,1:T(4,128)(4,1)S(1)}, pred[32,4]{0,1:T(4,128)(4,1)}, u32[]{:S(2)}) copy-start(pred[32,4]{0,1:T(4,128)(4,1)} %iota_compare_fusion.1) | copy-start | bytes 388
  154.5 8.2 %copy-start.32 = (f32[6]{0:T(128)S(1)}, f32[6]{0:T(128)}, u32[]{:S(2)}) copy-start(f32[6]{0:T(128)} %param.34) | copy-start | bytes 76
  154.5 8.7 %copy-start.30 = (f32[6]{0:T(128)S(1)}, f32[6]{0:T(128)}, u32[]{:S(2)}) copy-start(f32[6]{0:T(128)} %exponential_negate_fusion) | copy-start | bytes 76
  154.5 9.1 %copy-start.5 = (bf16[32,3,256]{2,1,0:T(4,128)(2,1)S(1)}, bf16[32,3,256]{2,1,0:T(4,128)(2,1)}, u32[]{:S(2)}) copy-start(bf16[32,3,256]{2,1,0:T(4,128)(2,1)} %gather_fusion.2) | copy-start | bytes 147460
  154.5 9.1 %copy-start.16 = (pred[32]{0:T(512)(128)(4,1)S(1)}, pred[32]{0:T(512)(128)(4,1)}, u32[]{:S(2)}) copy-start(pred[32]{0:T(512)(128)(4,1)} %get-tuple-element.158) | copy-start | bytes 100
  154.6 9.1 %copy-start.17 = (pred[32]{0:T(512)(128)(4,1)S(1)}, pred[32]{0:T(512)(128)(4,1)}, u32[]{:S(2)}) copy-start(pred[32]{0:T(512)(128)(4,1)} %get-tuple-element.159) | copy-start | bytes 100
  154.6 9.1 %copy-start.18 = (pred[32]{0:T(512)(128)(4,1)S(1)}, pred[32]{0:T(512)(128)(4,1)}, u32[]{:S(2)}) copy-start(pred[32]{0:T(512)(128)(4,1)} %get-tuple-element.160) | copy-start | bytes 100
  154.6 9.1 %copy-start.19 = (pred[32]{0:T(512)(128)(4,1)S(1)}, pred[32]{0:T(512)(128)(4,1)}, u32[]{:S(2)}) copy-start(pred[32]{0:T(512)(128)(4,1)} %get-tuple-element.161) | copy-start | bytes 100
  154.6 10.0 %copy-start.2 = (bf16[32,7,384]{2,0,1:T(8,128)(2,1)S(1)}, bf16[32,7,384]{2,0,1:T(8,128)(2,1)}, u32[]{:S(2)}) copy-start(bf16[32,7,384]{2,0,1:T(8,128)(2,1)} %copy_dynamic-update-slice_fusion.1) | copy-start | bytes 516100
  154.6 47.3 %all-to-all-start = ((bf16[32,6,64,128]{3,2,1,0:T(8,128)(2,1)}), bf16[32,6,64,128]{3,2,1,0:T(8,128)(2,1)}, u32[]{:S(2)}, u32[]{:S(2)}) async-start(bf16[32,6,64,128]{3,2,1,0:T(8,128)(2,1)} %scatter_fusion), calls=%async_computation | async-start | bytes 6291456 | tf_op jit(solution)/shard_map/all_to_all | solution.py:136
  162.2 2.5 copy-start.25
  162.2 2.8 copy-start.20
  162.2 2.8 copy-start.21
  162.2 2.8 copy-start.22
  162.2 2.8 copy-start.23
  162.2 2.8 copy-start.28
  162.2 169.2 %reduce-scatter.2.cloned.1.call-start = ((), (), s32[]{:S(2)}) async-start(), calls=%async_computation.5 | async-start | bytes 442368 | tf_op jit(solution)/shard_map/reduce_scatter | solution.py:209
  162.3 3.0 copy-start.3
  206.5 16.6 %copy-start.1 = (bf16[32,6,64,128]{3,2,1,0:T(8,128)(2,1)S(1)}, bf16[32,6,64,128]{3,2,1,0:T(8,128)(2,1)}, u32[]{:S(2)}) copy-start(bf16[32,6,64,128]{3,2,1,0:T(8,128)(2,1)} %gather_fusion) | copy-start | bytes 9437188
  258.7 21.4 %copy-start.29 = (f32[6]{0:T(128)S(1)}, f32[6]{0:T(128)}, u32[]{:S(2)}) copy-start(f32[6]{0:T(128)} %param.36) | copy-start | bytes 76
  258.7 36.2 %copy-start.26 = (f32[384]{0:T(512)S(1)}, f32[384]{0:T(512)}, u32[]{:S(2)}) copy-start(f32[384]{0:T(512)} %param.37) | copy-start | bytes 4612
  296.3 35.2 %copy-start.7 = (bf16[16,1536]{1,0:T(8,128)(2,1)S(1)}, bf16[16,1536]{1,0:T(8,128)(2,1)}, u32[]{:S(2)}) copy-start(bf16[16,1536]{1,0:T(8,128)(2,1)} %param.26) | copy-start | bytes 147460
Sparse Core Ops, SparseCore 0:
  15.1 52.6 all-gather.1
  296.4 35.0 reduce-scatter.1
